TPU v7x, 128 devices: a whole 4x4x4 slice. The times are simulated.
128 devices in a mesh: seq: 16 (over z, y), tensor: 8 (over x, core).
Axes of the slice: x: 4, y: 4, z: 4, core: 2. Of those that a mesh axis runs over, the one named last changes fastest.
Arguments:
- hidden_in: float32 [4096, 3840], P('seq'), may hold values from -6 to 6
- query_proj: float32 [3840, 4096], P(None, 'tensor'), may hold values from -0.09375 to 0.09375
- key_proj: float32 [3840, 2048], P(None, 'tensor'), may hold values from -0.09375 to 0.09375
- value_proj: float32 [3840, 2048], P(None, 'tensor'), may hold values from -0.09375 to 0.09375
- query_gain: float32 [256], replicated, may hold values from 0.1 to 1.9
- key_gain: float32 [256], replicated, may hold values from 0.1 to 1.9
- segment_ids: int32 [4096], replicated, may hold values from 0 to 3, never falling along the last dimension, each value on 1 to 2048 neighbouring positions
- grad_out: float32 [4096, 4096], P('seq', 'tensor'), may hold values from -6 to 6
Outputs:
- attended: float32 [4096, 4096], P('seq', 'tensor')
- grad_input: float32 [4096, 3840], P('seq', 'tensor')
- grad_query: float32 [3840, 4096], P('seq', 'tensor')
- grad_key: float32 [3840, 2048], P('seq', 'tensor')
- grad_value: float32 [3840, 2048], P('seq', 'tensor')
Inputs may be any that keep to these rules, and one draw needn't show every extreme that they name: `segment_ids`: segment ids never fall along the transcript; each of the 4 documents holds 1 to 2048 tokens and one holds exactly 2048.
All inputs are finite; a program needn't handle non-finite values.
Results may differ from a plain program's by a relative error of at most 0.0003.
Values sent between devices are 32-bit elements; how exact they have to be, the bound alone decides.
A program may use at most 128 MiB of HBM per device.

v0:
```python
import functools

import jax
import jax.numpy as jnp
from jax import lax
from jax.experimental import pallas as pl
from jax.experimental.pallas import tpu as pltpu
from jax.sharding import PartitionSpec as P

MESH = pl.DeviceIdType.MESH
WINDOW = 1024
EPS = 1e-06
T = 256
H = 256
D = 3840
NCH = 5
CH = D // NCH
F32, BF16 = jnp.float32, jnp.bfloat16

NN = (((1,), (0,)), ((), ()))
NT = (((1,), (1,)), ((), ()))
TN = (((0,), (0,)), ((), ()))


def split(value):
    high = value.astype(BF16)
    return high, (value - high.astype(F32)).astype(BF16)


def product(left, right, dims):
    (lh, ll), (rh, rl) = left, right
    dot = functools.partial(lax.dot_general, dimension_numbers=dims, preferred_element_type=F32)
    return dot(lh, rh) + (dot(lh, rl) + dot(ll, rh))


def rotate(u, cos, sin):
    a, b = u[:, :128], u[:, 128:]
    return jnp.concatenate([a * cos - b * sin, b * cos + a * sin], axis=1)


def unrotate(u, cos, sin):
    a, b = u[:, :128], u[:, 128:]
    return jnp.concatenate([a * cos + b * sin, b * cos - a * sin], axis=1)


def inv_rms(x):
    return lax.rsqrt(jnp.mean(x * x, axis=1, keepdims=True) + EPS)


def norm_back(x, gain, d_norm):
    r = inv_rms(x)
    gd = d_norm * gain
    return r * gd - x * (r * r * r) * jnp.mean(x * gd, axis=1, keepdims=True)


def kernel(
    hid_h, wq_h, wk_h, wv_h, grad_h, gains, seg, cos_r, sin_r,
    att_o, gin_o, gq_o, gk_o, gv_o,
    hid, wq, wk, wv, grad, raw, q2, kv, wt, dpt, dqt, contrib, rkv, prev, zr,
    hz, ht_h, ht_l, dc, part, rpart, term, r1, r2,
    lsem, kv_s, kv_r, hz_s, hz_r, hc_s, hc_r, cb_s, cb_r, pz_s, pz_r, dc_s, dc_r, pt_s, pt_r, t1_s, t1_r, t2_s, t2_r,
):
    s = lax.axis_index("seq")
    t = lax.axis_index("tensor")
    z, y = s // 4, lax.rem(s, 4)
    x, c = t // 2, lax.rem(t, 2)

    def at_z(d):
        return (lax.rem(z + d + 4, 4) * 4 + y, t)

    def at_y(d):
        return (z * 4 + lax.rem(y + d + 4, 4), t)

    def at_x(d):
        return (s, lax.rem(x + d + 4, 4) * 2 + c)

    mate = (s, x * 2 + 1 - c)

    def remote(src, dst, ssem, rsem, dev):
        return pltpu.make_async_remote_copy(
            src_ref=src, dst_ref=dst, send_sem=ssem, recv_sem=rsem, device_id=dev, device_id_type=MESH
        )

    barrier = pltpu.get_barrier_semaphore()
    partners = [at_z(1), at_z(2), at_z(3), at_y(1), at_y(2), at_y(3), at_x(1), at_x(2), at_x(3), mate]
    for dev in partners:
        pl.semaphore_signal(barrier, inc=1, device_id=dev, device_id_type=MESH)

    def columns(i):
        return pl.ds(pl.multiple_of(i * CH, CH), CH)

    def local_copy(j, i):
        if j == 0:
            return pltpu.make_async_copy(hid_h.at[:, columns(i)], hid.at[:, columns(i)], lsem.at[0, i])
        src, dst = ((wk_h, wk), (wv_h, wv), (wq_h, wq))[j - 1]
        return pltpu.make_async_copy(src.at[columns(i)], dst.at[columns(i)], lsem.at[j, i])

    for i in range(NCH):
        local_copy(0, i).start()
        local_copy(1, i).start()
    for j in (2, 3):
        for i in range(NCH):
            local_copy(j, i).start()
    grad_copy = pltpu.make_async_copy(grad_h, grad, lsem.at[4, 0])
    grad_copy.start()

    cos, sin = cos_r[...], sin_r[...]
    q_gain, k_gain = gains[0:1, :], gains[1:2, :]

    def project(j, weight, col, load_hid, load_w):
        def step(i, acc):
            if load_hid:
                local_copy(0, i).wait()
            if load_w:
                local_copy(j, i).wait()
            left = split(hid[:, columns(i)])
            right = split(weight[columns(i), col : col + H])
            return acc + product(left, right, NN)

        return lax.fori_loop(0, NCH, step, jnp.zeros((T, H), F32))

    def zhop(kind):
        return remote(kv.at[0, kind], kv.at[4, kind], kv_s.at[3, kind], kv_r.at[3, kind], at_z(1))

    def yhop(d, kind):
        return remote(
            kv.at[4 * ((y + d) // 4), kind], kv.at[d, kind], kv_s.at[d - 1, kind], kv_r.at[d - 1, kind], at_y(d)
        )

    def send_own(kind):
        zhop(kind).start()
        for d in (1, 2, 3):
            @pl.when(y + d < 4)
            def _():
                yhop(d, kind).start()

    def send_prev(kind):
        zhop(kind).wait_recv()
        for d in (1, 2, 3):
            @pl.when(y + d >= 4)
            def _():
                yhop(d, kind).start()

    key_raw = project(1, wk, 0, True, True)
    raw[2] = key_raw
    kv[0, 0] = rotate(key_raw * inv_rms(key_raw) * k_gain, cos, sin)
    pl.semaphore_wait(barrier, len(partners))
    send_own(0)
    kv[0, 1] = project(2, wv, 0, False, True)
    send_own(1)

    def query(h, load):
        q_raw = project(3, wq, h * H, False, load)
        raw[h] = q_raw
        q2[h * T : (h + 1) * T, :] = rotate(q_raw * inv_rms(q_raw) * q_gain, cos, sin) * (H ** -0.5)

    query(0, True)
    send_prev(0)
    query(1, False)
    send_prev(1)
    grad_copy.wait()

    half = pl.ds(pl.multiple_of(c * 128, 128), 128)

    def first_col(zz):
        return pl.ds(pl.multiple_of(((15 * zz) // 2) * 128, 128), 1024)

    def hidden_copy(d):
        zz = lax.rem(z + d, 4)
        return remote(hid.at[half, first_col(zz)], hz.at[d - 1, half], hz_s.at[d - 1], hz_r.at[d - 1], at_z(d))

    def hidden_mate(d):
        return remote(hz.at[d - 1, half], hz.at[d - 1, half], hc_s.at[d - 1], hc_r.at[d - 1], mate)

    for d in (1, 2, 3):
        hidden_copy(d).start()

    def q_pair():
        return split(q2[...])

    def g_pair():
        return split(jnp.concatenate([grad[:, :H], grad[:, H:]], axis=0))

    row = lax.broadcasted_iota(jnp.int32, (T, 2 * T), 0)
    col = lax.rem(lax.broadcasted_iota(jnp.int32, (T, 2 * T), 1), T)
    seg_q = seg[pl.ds(s, 1), :]
    seg_q = jnp.concatenate([seg_q, seg_q], axis=1)

    def forward(d, total, delta, out_t):
        blk = lax.rem(s - d + 16, 16)
        seg_k = jnp.broadcast_to(seg[pl.ds(blk, 1), :], (T, T)).T
        seg_k = jnp.concatenate([seg_k, seg_k], axis=1)
        dist = 256 * d + col - row
        allowed = (dist >= 0) & (dist < WINDOW) & (seg_k == seg_q) & (s - d >= 0)
        scores = product(split(kv[d, 0]), q_pair(), NT)
        weights = jnp.where(allowed, jnp.exp(scores), 0.0)
        wt[d] = weights
        v_pair = split(kv[d, 1])
        d_shares = product(v_pair, g_pair(), NT)
        dpt[d] = d_shares
        total = total + jnp.sum(weights, axis=0, keepdims=True)
        delta = delta + jnp.sum(weights * d_shares, axis=0, keepdims=True)
        return total, delta, out_t + product(v_pair, split(weights), TN)

    zero_row = jnp.zeros((1, 2 * T), F32)
    dqt[...] = jnp.zeros((H, 2 * T), F32)
    total, delta = zero_row, zero_row
    for d in (0, 4, 1, 3, 2):
        if d in (1, 2, 3):
            yhop(d, 0).wait_recv()
            yhop(d, 1).wait_recv()
        total, delta, out_t = forward(d, total, delta, dqt[...])
        dqt[...] = out_t
    inverse = 1.0 / total
    delta = delta * inverse
    attended = (dqt[...] * inverse).T
    att_o[:, :H] = attended[:T]
    att_o[:, H:] = attended[T:]

    def back_copy(d, kind):
        return remote(contrib.at[d, kind], rkv.at[d - 1, kind], cb_s.at[d - 1, kind], cb_r.at[d - 1, kind], at_y(-d))

    for d in (2, 1, 3, 4, 0):
        shares = wt[d] * inverse
        wt[d] = shares
        contrib[d, 1] = product(split(shares), g_pair(), NN)
        if d in (1, 2, 3):
            back_copy(d, 1).start()
    d_q = jnp.zeros((H, 2 * T), F32)
    for d in (2, 1, 3, 4, 0):
        d_scores = split(wt[d] * (dpt[d] - delta))
        contrib[d, 0] = product(d_scores, q_pair(), NN)
        if d in (1, 2, 3):
            back_copy(d, 0).start()
        d_q = d_q + product(split(kv[d, 0]), d_scores, TN)
    d_q = d_q.T * (H ** -0.5)

    def gather(g, d):
        w = 2 * H if g == 0 else H
        cols = pl.ds(0 if g == 0 else (g + 1) * H, w)
        return remote(dc.at[0, :, cols], dc.at[d, :, cols], dc_s.at[g, d - 1], dc_r.at[g, d - 1], at_z(d))

    for h in (0, 1):
        dc[0, :, h * H : (h + 1) * H] = norm_back(raw[h], q_gain, unrotate(d_q[h * T : (h + 1) * T], cos, sin))
    for d in (1, 2, 3):
        gather(0, d).start()

    for d in (1, 2, 3):
        hidden_copy(d).wait_recv()
        hidden_mate(d).start()

    def transpose_into(d, read):
        def step(i, carry):
            lanes = pl.multiple_of(i * 256, 256)
            high, low = split(read(lanes).T)
            ht_h[pl.ds(lanes, 256), d * T : (d + 1) * T] = high
            ht_l[pl.ds(lanes, 256), d * T : (d + 1) * T] = low
            return carry

        lax.fori_loop(0, 4, step, 0)

    base = ((15 * z) // 2) * 128
    transpose_into(0, lambda lanes: hid[:, pl.ds(pl.multiple_of(base + lanes, 128), 256)])
    for d in (1, 2, 3):
        hidden_mate(d).wait_recv()
        transpose_into(d, lambda lanes: hz[d - 1, :, pl.ds(lanes, 256)])

    def prev_copy(kind):
        return remote(prev.at[kind], zr.at[kind], pz_s.at[kind], pz_r.at[kind], at_z(-1))

    own = [None, None]
    for kind in (1, 0):
        mine, before = contrib[0, kind], contrib[4, kind]
        for d in (1, 2, 3):
            back_copy(d, kind).wait_recv()
            got = rkv[d - 1, kind]
            inside = jnp.where(y + d < 4, 1.0, 0.0).astype(F32)
            mine = mine + inside * got
            before = before + (1.0 - inside) * got
        prev[kind] = before
        contrib[0, kind] = mine
        prev_copy(kind).start()

    off = lax.rem(z, 2) * 64

    def rows_of(yy):
        return pl.ds(pl.multiple_of(off + 240 * yy, 16), 240)

    def scatter(g, d):
        return remote(part.at[d, g], rpart.at[d - 1, g], pt_s.at[g, d - 1], pt_r.at[g, d - 1], at_y(d))

    def partial(g):
        def blocks(k):
            return split(dc[k, :, g * H : (g + 1) * H])

        pieces = [blocks(k) for k in range(4)]
        right = tuple(jnp.concatenate([p[i] for p in pieces], axis=0) for i in (0, 1))
        for d in (1, 2, 3, 0):
            rows = rows_of(lax.rem(y + d, 4))
            part[d, g] = product((ht_h[rows, :], ht_l[rows, :]), right, NN)
            if d:
                scatter(g, d).start()

    for d in (1, 2, 3):
        gather(0, d).wait_recv()
    partial(0)
    partial(1)

    prev_copy(1).wait_recv()
    dc[0, :, 3 * H : 4 * H] = contrib[0, 1] + zr[1]
    for d in (1, 2, 3):
        gather(2, d).start()
    prev_copy(0).wait_recv()
    d_key = unrotate(contrib[0, 0] + zr[0], cos, sin)
    dc[0, :, 2 * H : 3 * H] = norm_back(raw[2], k_gain, d_key)
    for d in (1, 2, 3):
        gather(1, d).start()

    d_own = [split(dc[0, :, g * H : (g + 1) * H]) for g in range(4)]
    weights = [(wq, 0), (wq, H), (wk, 0), (wv, 0)]

    def input_term(tt):
        rows = pl.ds(pl.multiple_of(tt * 480, 32), 480)
        acc = None
        for g in range(4):
            w, first = weights[g]
            one = product(d_own[g], split(w[rows, first : first + H]), NT)
            acc = one if acc is None else acc + one
        return acc

    def core_copy(k):
        return remote(term.at[1, k], r1.at[k], t1_s.at[k], t1_r.at[k], mate)

    def x_copy(d):
        return remote(term.at[0, d], r2.at[d - 1], t2_s.at[d - 1], t2_r.at[d - 1], at_x(d))

    for k in (1, 2, 3, 0):
        term[1, k] = input_term(2 * lax.rem(x + k, 4) + 1 - c)
        core_copy(k).start()
    for k in (1, 2, 3, 0):
        mine = input_term(2 * lax.rem(x + k, 4) + c)
        core_copy(k).wait_recv()
        term[0, k] = mine + r1[k]
        if k:
            x_copy(k).start()

    for d in (1, 2, 3):
        gather(2, d).wait_recv()
    partial(3)
    for d in (1, 2, 3):
        gather(1, d).wait_recv()
    partial(2)

    total_in = term[0, 0]
    for k in (1, 2, 3):
        x_copy(k).wait_recv()
        total_in = total_in + r2[k - 1]
    gin_o[...] = total_in

    for g in (0, 1, 3, 2):
        acc = part[0, g]
        for d in (1, 2, 3):
            scatter(g, d).wait_recv()
            acc = acc + rpart[d - 1, g]
        if g < 2:
            gq_o[:, g * H : (g + 1) * H] = acc
        elif g == 2:
            gk_o[...] = acc
        else:
            gv_o[...] = acc

    for kind in (0, 1):
        zhop(kind).wait_send()
        prev_copy(kind).wait_send()
        for d in (1, 2, 3):
            yhop(d, kind).wait_send()
            back_copy(d, kind).wait_send()
    for d in (1, 2, 3):
        hidden_copy(d).wait_send()
        hidden_mate(d).wait_send()
        x_copy(d).wait_send()
        for g in range(3):
            gather(g, d).wait_send()
        for g in range(4):
            scatter(g, d).wait_send()
    for k in range(4):
        core_copy(k).wait_send()


def local(hidden_in, query_proj, key_proj, value_proj, query_gain, key_gain, segment_ids, grad_out):
    s = lax.axis_index("seq")
    positions = s * T + jnp.arange(T, dtype=jnp.int32)
    exponent = 2.0 * jnp.arange(H // 2).astype(F32) / H
    frequency = 10000.0 ** (-exponent)
    angles = positions.astype(F32)[:, None] * frequency[None, :]
    gains = jnp.stack([query_gain, key_gain])
    vmem = pl.BlockSpec(memory_space=pltpu.VMEM)
    hbm = pl.BlockSpec(memory_space=pl.ANY)
    V, S = pltpu.VMEM, pltpu.SemaphoreType.DMA
    shape = jax.ShapeDtypeStruct
    return pl.pallas_call(
        kernel,
        out_shape=(
            shape((T, 512), F32), shape((T, 480), F32), shape((240, 512), F32), shape((240, 256), F32), shape((240, 256), F32),
        ),
        in_specs=[hbm] * 5 + [vmem] * 4,
        out_specs=(vmem,) * 5,
        scratch_shapes=[
            V((T, D), F32), V((D, 512), F32), V((D, 256), F32), V((D, 256), F32), V((T, 512), F32),
            V((3, T, H), F32), V((2 * T, H), F32), V((5, 2, T, H), F32), V((5, T, 2 * T), F32), V((5, T, 2 * T), F32),
            V((H, 2 * T), F32), V((5, 2, T, H), F32), V((3, 2, T, H), F32), V((2, T, H), F32), V((2, T, H), F32),
            V((3, T, 1024), F32), V((1024, 1024), BF16), V((1024, 1024), BF16), V((4, T, 1024), F32),
            V((4, 4, 240, H), F32), V((3, 4, 240, H), F32), V((2, 4, T, 480), F32), V((4, T, 480), F32), V((3, T, 480), F32),
            S((5, NCH)), S((4, 2)), S((4, 2)), S((3,)), S((3,)), S((3,)), S((3,)), S((3, 2)), S((3, 2)), S((2,)), S((2,)),
            S((3, 3)), S((3, 3)), S((4, 3)), S((4, 3)), S((4,)), S((4,)), S((3,)), S((3,)),
        ],
        compiler_params=pltpu.CompilerParams(collective_id=0, has_side_effects=True, vmem_limit_bytes=63 << 20),
        cost_estimate=pl.CostEstimate(flops=24_000_000_000, bytes_accessed=40_000_000, transcendentals=700_000),
    )(
        hidden_in, query_proj, key_proj, value_proj, grad_out,
        gains, segment_ids.reshape(16, T), jnp.cos(angles), jnp.sin(angles),
    )


def solution(mesh):
    return jax.shard_map(
        local,
        mesh=mesh,
        in_specs=(
            P("seq", None), P(None, "tensor"), P(None, "tensor"), P(None, "tensor"), P(), P(), P(), P("seq", "tensor"),
        ),
        out_specs=(P("seq", "tensor"),) * 5,
        check_vma=False,
    )
```

profile of v0, /device:TPU:0, one launch (start us, length us, event | category | flops | bytes accessed | tf_op | source)
XLA Modules:
  0.0 130.7 jit_solution(5766701137563899707)
XLA Ops:
  0.7 1.3 pad_maximum_fusion.gains
  1.9 1.3 %reshape.25.seg = s32[16,256]{1,0:T(8,128)} reshape(s32[4096]{0:T(1024)} %param.14) | data formatting | bytes 32768 | tf_op jit(solution)/shard_map/reshape | solution.py:421
  3.3 1.2 multiply_sine_fusion
  4.5 117.1 %shard_map.119 = (f32[256,512]{1,0:T(8,128)}, f32[256,480]{1,0:T(8,128)}, f32[240,512]{1,0:T(8,128)}, f32[240,256]{1,0:T(8,128)}, f32[240,256]{1,0:T(8,128)}) custom-call(f32[256,3840]{1,0:T(8,128)} %hid_h.1, f32[3840,512]{1,0:T(8,128)} %wq_h.1, f32[3840,256]{1,0:T(8,128)} %wk_h.1, f32[3840,256]{1,0:T(8,128)} %wv_h.1, f32[256,512]{1,0:T(8,128)} %grad_h.1, ...), custom_call_target="tpu_custom_call" | custom-call | flops 24000000000 | bytes 40000000 | tf_op jit(solution)/shard_map/pallas_call | solution.py:401
  121.6 2.0 %copy.13 = f32[256,480]{0,1:T(8,128)} copy(f32[256,480]{1,0:T(8,128)} %get-tuple-element.6) | data formatting | bytes 983040 | tf_op jit(solution)/shard_map/pallas_call | solution.py:401
  123.6 1.9 %copy.18 = f32[256,512]{1,0:T(8,128)} copy(f32[256,512]{1,0:T(8,128)} %get-tuple-element.17) | data formatting | bytes 1048576
  125.5 1.8 %copy.19 = f32[240,512]{1,0:T(8,128)} copy(f32[240,512]{1,0:T(8,128)} %get-tuple-element.19) | data formatting | bytes 983040
  127.4 1.7 %copy.20 = f32[240,256]{1,0:T(8,128)} copy(f32[240,256]{1,0:T(8,128)} %get-tuple-element.20) | data formatting | bytes 491520
  129.0 1.7 %copy.21 = f32[240,256]{1,0:T(8,128)} copy(f32[240,256]{1,0:T(8,128)} %get-tuple-element.21) | data formatting | bytes 491520
  (2 shorter events, 0.0 us)
where the time goes:
time: 133 us; the launch traced here: 131 us
  Pallas kernels  117 us (88%)
  local copies, waits for them, and re-layouts  10.4 us (8%)
  other arithmetic  2.53 us (2%)
    pallas_call x1, Pallas kernels, local(): pl.pallas_call(kernel, out_shape=(shape((T, 512), F32), shape((T, 480), F...  117 us
    unnamed x4, local copies, waits for them, and re-layouts  7.01 us

commit v1 on v0

v1 whole, which is shorter than its diff:
```python
import functools

import jax
import jax.numpy as jnp
import numpy as np
from jax import lax
from jax.experimental import pallas as pl
from jax.experimental.pallas import tpu as pltpu
from jax.sharding import PartitionSpec as P

MESH = pl.DeviceIdType.MESH
WINDOW = 1024
EPS = 1e-06
T = 256
H = 256
D = 3840
NCH = 5
CH = D // NCH
F32, BF16 = jnp.float32, jnp.bfloat16

NN = (((1,), (0,)), ((), ()))
NT = (((1,), (1,)), ((), ()))
TN = (((0,), (0,)), ((), ()))


def split(value):
    high = value.astype(BF16)
    return high, (value - high.astype(F32)).astype(BF16)


def product(left, right, dims):
    (lh, ll), (rh, rl) = left, right
    dot = functools.partial(lax.dot_general, dimension_numbers=dims, preferred_element_type=F32)
    return dot(lh, rh) + (dot(lh, rl) + dot(ll, rh))


def rotate(u, cos, sin):
    a, b = u[:, :128], u[:, 128:]
    return jnp.concatenate([a * cos - b * sin, b * cos + a * sin], axis=1)


def unrotate(u, cos, sin):
    a, b = u[:, :128], u[:, 128:]
    return jnp.concatenate([a * cos + b * sin, b * cos - a * sin], axis=1)


def inv_rms(x):
    return lax.rsqrt(jnp.mean(x * x, axis=1, keepdims=True) + EPS)


def norm_back(x, gain, d_norm):
    r = inv_rms(x)
    gd = d_norm * gain
    return r * gd - x * (r * r * r) * jnp.mean(x * gd, axis=1, keepdims=True)


class Links:
    def __init__(self, send_sems, recv_sems):
        self.sems = send_sems, recv_sems
        self.copies = {}

    def add(self, name, src, dst, device):
        i = len(self.copies)
        self.copies[name] = pltpu.make_async_remote_copy(
            src_ref=src, dst_ref=dst, send_sem=self.sems[0].at[i], recv_sem=self.sems[1].at[i],
            device_id=device, device_id_type=MESH,
        )

    def start(self, *name):
        self.copies[name].start()

    def arrived(self, *name):
        self.copies[name].wait_recv()

    def finish(self):
        for copy in self.copies.values():
            copy.wait_send()


COPIES = 64


def kernel(
    hid_h, wq_h, wk_h, wv_h, grad_h, q_gain_r, k_gain_r, seg, freq_r,
    att_o, gin_o, gq_o, gk_o, gv_o,
    hid, wq, wk, wv, grad, raw, q2, kv, wt, dpt, dqt, contrib, rkv, prev, zr,
    hz, ht_h, ht_l, dc, part, fwd, rpart, term, r1, r2, lsem, send_sems, recv_sems,
):
    s = lax.axis_index("seq")
    t = lax.axis_index("tensor")
    z, y = s // 4, lax.rem(s, 4)
    x, c = t // 2, lax.rem(t, 2)

    def at_z(d):
        return (lax.rem(z + d + 4, 4) * 4 + y, t)

    def at_y(d):
        return (z * 4 + lax.rem(y + d + 4, 4), t)

    def at_x(d):
        return (s, lax.rem(x + d + 4, 4) * 2 + c)

    mate = (s, x * 2 + 1 - c)
    barrier = pltpu.get_barrier_semaphore()
    partners = [at_z(1), at_z(2), at_z(3), at_y(1), at_y(2), at_y(3), at_x(1), at_x(2), at_x(3), mate]
    for dev in partners:
        pl.semaphore_signal(barrier, inc=1, device_id=dev, device_id_type=MESH)

    links = Links(send_sems, recv_sems)
    half = pl.ds(pl.multiple_of(c * 128, 128), 128)

    def first_col(zz):
        return ((15 * zz) // 2) * 128

    for kind in (0, 1):
        links.add(("kv", 4, kind), kv.at[0, kind], kv.at[4, kind], at_z(1))
        links.add(("prev", kind), prev.at[kind], zr.at[kind], at_z(-1))
        for d in (1, 2, 3):
            links.add(("kv", d, kind), kv.at[4 * ((y + d) // 4), kind], kv.at[d, kind], at_y(d))
            links.add(("back", d, kind), contrib.at[d, kind], rkv.at[d - 1, kind], at_y(-d))
    for d in (1, 2, 3):
        cols = pl.ds(pl.multiple_of(first_col(lax.rem(z + d, 4)), 128), 1024)
        links.add(("hid", d), hid.at[half, cols], hz.at[d - 1, half], at_z(d))
        links.add(("hid_mate", d), hz.at[d - 1, half], hz.at[d - 1, half], mate)
        links.add(("x", d), term.at[0, d], r2.at[d - 1], at_x(d))
    for k in range(4):
        links.add(("core", k), term.at[1, k], r1.at[k], mate)
    spans = {"q": pl.ds(0, 2 * H), "k": pl.ds(2 * H, H), "v": pl.ds(3 * H, H)}
    for g, cols in spans.items():
        links.add(("dc", g, 1), dc.at[0, :, cols], dc.at[1, :, cols], at_z(1))
        links.add(("dc", g, 3), dc.at[0, :, cols], dc.at[3, :, cols], at_z(-1))
        links.add(("dc2", g, 1), dc.at[1, :128, cols], dc.at[2, :128, cols], at_z(1))
        links.add(("dc2", g, 3), dc.at[3, 128:, cols], dc.at[2, 128:, cols], at_z(-1))
    for g in range(4):
        links.add(("fwd", g, 1), part.at[2, g, :120], fwd.at[0, g], at_y(1))
        links.add(("fwd", g, 3), part.at[2, g, 120:], fwd.at[1, g], at_y(-1))
        links.add(("sum", g, 1), part.at[1, g], rpart.at[0, g], at_y(1))
        links.add(("sum", g, 3), part.at[3, g], rpart.at[1, g], at_y(-1))

    def columns(i):
        return pl.ds(pl.multiple_of(i * CH, CH), CH)

    def local_copy(j, i):
        if j == 0:
            return pltpu.make_async_copy(hid_h.at[:, columns(i)], hid.at[:, columns(i)], lsem.at[0, i])
        src, dst = ((wk_h, wk), (wv_h, wv), (wq_h, wq))[j - 1]
        return pltpu.make_async_copy(src.at[columns(i)], dst.at[columns(i)], lsem.at[j, i])

    for i in range(NCH):
        local_copy(0, i).start()
        local_copy(1, i).start()
    for j in (2, 3):
        for i in range(NCH):
            local_copy(j, i).start()
    grad_copy = pltpu.make_async_copy(grad_h, grad, lsem.at[4, 0])
    grad_copy.start()

    place = (s * T + lax.broadcasted_iota(jnp.int32, (T, H // 2), 0)).astype(F32)
    angle = place * freq_r[...]
    cos, sin = jnp.cos(angle), jnp.sin(angle)
    q_gain, k_gain = q_gain_r[...], k_gain_r[...]

    def project(j, weight, col, load_hid, load_w):
        def step(i, acc):
            if load_hid:
                local_copy(0, i).wait()
            if load_w:
                local_copy(j, i).wait()
            left = split(hid[:, columns(i)])
            right = split(weight[columns(i), col : col + H])
            return acc + product(left, right, NN)

        return lax.fori_loop(0, NCH, step, jnp.zeros((T, H), F32))

    def send_own(kind):
        links.start("kv", 4, kind)
        for d in (1, 2, 3):
            @pl.when(y + d < 4)
            def _():
                links.start("kv", d, kind)

    def send_prev(kind):
        links.arrived("kv", 4, kind)
        for d in (1, 2, 3):
            @pl.when(y + d >= 4)
            def _():
                links.start("kv", d, kind)

    key_raw = project(1, wk, 0, True, True)
    raw[2] = key_raw
    kv[0, 0] = rotate(key_raw * inv_rms(key_raw) * k_gain, cos, sin)
    pl.semaphore_wait(barrier, len(partners))
    send_own(0)
    kv[0, 1] = project(2, wv, 0, False, True)
    send_own(1)

    def query(h, load):
        q_raw = project(3, wq, h * H, False, load)
        raw[h] = q_raw
        q2[h * T : (h + 1) * T, :] = rotate(q_raw * inv_rms(q_raw) * q_gain, cos, sin) * (H ** -0.5)

    query(0, True)
    send_prev(0)
    query(1, False)
    send_prev(1)
    grad_copy.wait()

    for d in (1, 2, 3):
        links.start("hid", d)

    def q_pair():
        return split(q2[...])

    def g_pair():
        return split(jnp.concatenate([grad[:, :H], grad[:, H:]], axis=0))

    row = lax.broadcasted_iota(jnp.int32, (T, 2 * T), 0)
    col = lax.rem(lax.broadcasted_iota(jnp.int32, (T, 2 * T), 1), T)

    def segments(blk):
        return seg[:, pl.ds(pl.multiple_of(blk * T, T), T)]

    seg_q = segments(s)
    seg_q = jnp.concatenate([seg_q, seg_q], axis=1)

    def forward(d, total, delta):
        seg_k = jnp.broadcast_to(segments(lax.rem(s - d + 16, 16)), (T, T)).T
        seg_k = jnp.concatenate([seg_k, seg_k], axis=1)
        dist = 256 * d + col - row
        allowed = (dist >= 0) & (dist < WINDOW) & (seg_k == seg_q) & (s - d >= 0)
        scores = product(split(kv[d, 0]), q_pair(), NT)
        weights = jnp.where(allowed, jnp.exp(scores), 0.0)
        wt[d] = weights
        d_shares = product(split(kv[d, 1]), g_pair(), NT)
        dpt[d] = d_shares
        total = total + jnp.sum(weights, axis=0, keepdims=True)
        delta = delta + jnp.sum(weights * d_shares, axis=0, keepdims=True)
        return total, delta

    total = delta = jnp.zeros((1, 2 * T), F32)
    for d in (0, 4, 1, 3, 2):
        if d in (1, 2, 3):
            links.arrived("kv", d, 0)
            links.arrived("kv", d, 1)
        total, delta = forward(d, total, delta)
    inverse = 1.0 / total
    delta = delta * inverse

    def back_values(d):
        shares = wt[d] * inverse
        wt[d] = shares
        contrib[d, 1] = product(split(shares), g_pair(), NN)

    def back_keys(d, first):
        d_scores = split(wt[d] * (dpt[d] - delta))
        contrib[d, 0] = product(d_scores, q_pair(), NN)
        if d in (1, 2, 3):
            links.start("back", d, 0)
        more = product(split(kv[d, 0]), d_scores, TN)
        dqt[...] = more if first else dqt[...] + more

    for d in (2, 1, 3):
        back_values(d)
        links.start("back", d, 1)
    for d in (2, 1, 3):
        back_keys(d, d == 2)
    for d in (4, 0):
        back_values(d)
        back_keys(d, False)
    d_q = dqt[...].T * (H ** -0.5)
    for h in (0, 1):
        dc[0, :, h * H : (h + 1) * H] = norm_back(raw[h], q_gain, unrotate(d_q[h * T : (h + 1) * T], cos, sin))

    def spread(g):
        links.start("dc", g, 1)
        links.start("dc", g, 3)

    def spread_on(g):
        for d in (1, 3):
            links.arrived("dc", g, d)
            links.start("dc2", g, d)

    def gathered(g):
        for d in (1, 3):
            links.arrived("dc2", g, d)

    spread("q")

    out_t = None
    for d in range(5):
        more = product(split(kv[d, 1]), split(wt[d]), TN)
        out_t = more if out_t is None else out_t + more
    attended = out_t.T
    att_o[:, :H] = attended[:T]
    att_o[:, H:] = attended[T:]

    for d in (1, 2, 3):
        links.arrived("hid", d)
        links.start("hid_mate", d)

    def transpose_into(d, read):
        def step(i, carry):
            lanes = pl.multiple_of(i * 256, 256)
            high, low = split(read(lanes).T)
            ht_h[pl.ds(lanes, 256), d * T : (d + 1) * T] = high
            ht_l[pl.ds(lanes, 256), d * T : (d + 1) * T] = low
            return carry

        lax.fori_loop(0, 4, step, 0)

    base = first_col(z)
    transpose_into(0, lambda lanes: hid[:, pl.ds(pl.multiple_of(base + lanes, 128), 256)])
    for d in (1, 2, 3):
        links.arrived("hid_mate", d)
        transpose_into(d, lambda lanes: hz[d - 1, :, pl.ds(lanes, 256)])

    def collect(kind):
        mine, before = contrib[0, kind], contrib[4, kind]
        for d in (1, 2, 3):
            links.arrived("back", d, kind)
            got = rkv[d - 1, kind]
            inside = jnp.where(y + d < 4, 1.0, 0.0).astype(F32)
            mine = mine + inside * got
            before = before + (1.0 - inside) * got
        prev[kind] = before
        contrib[0, kind] = mine
        links.start("prev", kind)

    collect(1)
    spread_on("q")
    collect(0)

    off = lax.rem(z, 2) * 64

    def partial(g):
        pieces = [split(dc[k, :, g * H : (g + 1) * H]) for k in range(4)]
        right = tuple(jnp.concatenate([p[i] for p in pieces], axis=0) for i in (0, 1))
        for d in (2, 1, 3, 0):
            rows = pl.ds(pl.multiple_of(off + 240 * lax.rem(y + d, 4), 16), 240)
            part[d, g] = product((ht_h[rows, :], ht_l[rows, :]), right, NN)
            if d == 2:
                links.start("fwd", g, 1)
                links.start("fwd", g, 3)

    def pass_on(g):
        links.arrived("fwd", g, 1)
        part[1, g, :120] = part[1, g, :120] + fwd[0, g]
        links.start("sum", g, 1)
        links.arrived("fwd", g, 3)
        part[3, g, 120:] = part[3, g, 120:] + fwd[1, g]
        links.start("sum", g, 3)

    def summed(g):
        links.arrived("sum", g, 1)
        links.arrived("sum", g, 3)
        return part[0, g] + (rpart[0, g] + rpart[1, g])

    gathered("q")
    partial(0)
    partial(1)

    links.arrived("prev", 1)
    dc[0, :, 3 * H : 4 * H] = contrib[0, 1] + zr[1]
    spread("v")
    pass_on(0)
    pass_on(1)
    links.arrived("prev", 0)
    d_key = unrotate(contrib[0, 0] + zr[0], cos, sin)
    dc[0, :, 2 * H : 3 * H] = norm_back(raw[2], k_gain, d_key)
    spread("k")

    d_own = [split(dc[0, :, g * H : (g + 1) * H]) for g in range(4)]
    weights = [(wq, 0), (wq, H), (wk, 0), (wv, 0)]

    def input_term(tt):
        rows = pl.ds(pl.multiple_of(tt * 480, 32), 480)
        acc = None
        for g in range(4):
            w, first = weights[g]
            one = product(split(w[rows, first : first + H]), d_own[g], NT)
            acc = one if acc is None else acc + one
        return acc

    for k in (1, 2, 3, 0):
        term[1, k] = input_term(2 * lax.rem(x + k, 4) + 1 - c)
        links.start("core", k)
    spread_on("v")
    for k in (1, 2, 3, 0):
        mine = input_term(2 * lax.rem(x + k, 4) + c)
        links.arrived("core", k)
        term[0, k] = mine + r1[k]
        if k:
            links.start("x", k)
    spread_on("k")

    gathered("v")
    partial(3)
    gathered("k")
    partial(2)
    pass_on(3)
    pass_on(2)

    gq_o[:, :H] = summed(0)
    gq_o[:, H:] = summed(1)
    total_in = term[0, 0]
    for k in (1, 2, 3):
        links.arrived("x", k)
        total_in = total_in + r2[k - 1]
    gin_o[...] = total_in
    gv_o[...] = summed(3)
    gk_o[...] = summed(2)
    links.finish()


def hand_over(*refs):
    count = (len(refs) - 1) // 2
    copies = [pltpu.make_async_copy(refs[i], refs[count + i], refs[-1].at[i]) for i in range(count)]
    for copy in copies:
        copy.start()
    for copy in copies:
        copy.wait()


def local(hidden_in, query_proj, key_proj, value_proj, query_gain, key_gain, segment_ids, grad_out):
    frequency = np.power(10000.0, -2.0 * np.arange(H // 2) / H).astype(np.float32)[None, :]
    vmem = pl.BlockSpec(memory_space=pltpu.VMEM)
    hbm = pl.BlockSpec(memory_space=pl.ANY)
    V, S = pltpu.VMEM, pltpu.SemaphoreType.DMA
    shape = jax.ShapeDtypeStruct
    outs = (
        shape((T, 512), F32), shape((480, T), F32), shape((240, 512), F32), shape((240, 256), F32), shape((240, 256), F32),
    )
    results = pl.pallas_call(
        kernel,
        out_shape=outs,
        in_specs=[hbm] * 5 + [vmem] * 4,
        out_specs=(vmem,) * 5,
        scratch_shapes=[
            V((T, D), F32), V((D, 512), F32), V((D, 256), F32), V((D, 256), F32), V((T, 512), F32),
            V((3, T, H), F32), V((2 * T, H), F32), V((5, 2, T, H), F32), V((5, T, 2 * T), F32), V((5, T, 2 * T), F32),
            V((H, 2 * T), F32), V((5, 2, T, H), F32), V((3, 2, T, H), F32), V((2, T, H), F32), V((2, T, H), F32),
            V((3, T, 1024), F32), V((1024, 1024), BF16), V((1024, 1024), BF16), V((4, T, 1024), F32),
            V((4, 4, 240, H), F32), V((2, 4, 120, H), F32), V((2, 4, 240, H), F32),
            V((2, 4, 480, T), F32), V((4, 480, T), F32), V((3, 480, T), F32),
            S((5, NCH)), S((COPIES,)), S((COPIES,)),
        ],
        compiler_params=pltpu.CompilerParams(collective_id=0, has_side_effects=True, vmem_limit_bytes=63 << 20),
        cost_estimate=pl.CostEstimate(flops=24_000_000_000, bytes_accessed=40_000_000, transcendentals=700_000),
    )(
        hidden_in, query_proj, key_proj, value_proj, grad_out,
        query_gain.reshape(1, H), key_gain.reshape(1, H), segment_ids.reshape(1, -1), jnp.asarray(frequency),
    )
    attended, grad_in, grad_query, grad_key, grad_value = pl.pallas_call(
        hand_over, out_shape=outs, in_specs=[hbm] * 5, out_specs=(hbm,) * 5, scratch_shapes=[S((5,))],
    )(*results)
    return attended, grad_in.T, grad_query, grad_key, grad_value


def solution(mesh):
    return jax.shard_map(
        local,
        mesh=mesh,
        in_specs=(
            P("seq", None), P(None, "tensor"), P(None, "tensor"), P(None, "tensor"), P(), P(), P(), P("seq", "tensor"),
        ),
        out_specs=(P("seq", "tensor"),) * 5,
        check_vma=False,
    )
```

time: 133 us -> 180 us (1.35)
  Pallas kernels: 117 us -> 179 us
  local copies, waits for them, and re-layouts: 10.4 us -> 0 us
  other arithmetic: 2.53 us -> 0 us
    pallas_call x1 -> x2, Pallas kernels: 117 us -> 179 us  [the longest x1 117 us: local(): pl.pallas_call(kernel, out_shape=outs, in_specs=[hbm] * 5 + [vmem] * 4, o...]
    unnamed x4 -> x0, local copies, waits for them, and re-layouts: 7.01 us -> none
    pallas_call x1 -> x0, local copies, waits for them, and re-layouts: 2.01 us -> none  [local(): pl.pallas_call(kernel, out_shape=(shape((T, 512), F32), shape((T, 480), F...]
where the time goes in v1:
time: 180 us; the launch traced here: 179 us
  Pallas kernels  179 us (99%)
    pallas_call x1, Pallas kernels, local(): pl.pallas_call(kernel, out_shape=outs, in_specs=[hbm] * 5 + [vmem] * 4, o...  117 us
    pallas_call x1, Pallas kernels, local(): pl.pallas_call(hand_over, out_shape=outs, in_specs=[hbm] * 5, out_specs=(...  61.7 us

profile of v1, /device:TPU:0, one launch (start us, length us, event | category | flops | bytes accessed | tf_op | source)
XLA Modules:
  0.0 179.4 jit_solution(219793007695209424)
XLA Ops:
  0.6 116.9 %shard_map.128 = (f32[256,512]{1,0:T(8,128)}, f32[480,256]{1,0:T(8,128)}, f32[240,512]{1,0:T(8,128)}, f32[240,256]{1,0:T(8,128)}, f32[240,256]{1,0:T(8,128)}) custom-call(f32[256,3840]{1,0:T(8,128)} %hid_h.1, f32[3840,512]{1,0:T(8,128)} %wq_h.1, f32[3840,256]{1,0:T(8,128)} %wk_h.1, f32[3840,256]{1,0:T(8,128)} %wv_h.1, f32[256,512]{1,0:T(8,128)} %grad_h.1, ...), custom_call_target="tpu_custom_call" | custom-call | flops 24000000000 | bytes 40000000 | tf_op jit(solution)/shard_map/pallas_call | solution.py:433
  117.5 61.7 %shard_map.129 = (f32[256,512]{1,0:T(8,128)}, f32[480,256]{1,0:T(8,128)}, f32[240,512]{1,0:T(8,128)}, f32[240,256]{1,0:T(8,128)}, f32[240,256]{1,0:T(8,128)}) custom-call(f32[256,512]{1,0:T(8,128)} %get-tuple-element.15.refs_0_, f32[480,256]{1,0:T(8,128)} %get-tuple-element.16.refs_1_, f32[240,512]{1,0:T(8,128)} %get-tuple-element.17.refs_2_, ...), custom_call_target="tpu_custom_call" | custom-call | tf_op jit(solution)/shard_map/pallas_call | solution.py:453

commit v2 on v1

--- a/solution.py
+++ b/solution.py
@@ -413,12 +413,16 @@
 
 
 def hand_over(*refs):
-    count = (len(refs) - 1) // 2
-    copies = [pltpu.make_async_copy(refs[i], refs[count + i], refs[-1].at[i]) for i in range(count)]
-    for copy in copies:
-        copy.start()
-    for copy in copies:
-        copy.wait()
+    ins, outs, held, sems = refs[:5], refs[5:10], refs[10:15], refs[15]
+    loads = [pltpu.make_async_copy(ins[i], held[i], sems.at[0, i]) for i in range(5)]
+    stores = [pltpu.make_async_copy(held[i], outs[i], sems.at[1, i]) for i in range(5)]
+    for load in loads:
+        load.start()
+    for load, store in zip(loads, stores):
+        load.wait()
+        store.start()
+    for store in stores:
+        store.wait()
 
 
 def local(hidden_in, query_proj, key_proj, value_proj, query_gain, key_gain, segment_ids, grad_out):
@@ -451,7 +455,8 @@
         query_gain.reshape(1, H), key_gain.reshape(1, H), segment_ids.reshape(1, -1), jnp.asarray(frequency),
     )
     attended, grad_in, grad_query, grad_key, grad_value = pl.pallas_call(
-        hand_over, out_shape=outs, in_specs=[hbm] * 5, out_specs=(hbm,) * 5, scratch_shapes=[S((5,))],
+        hand_over, out_shape=outs, in_specs=[hbm] * 5, out_specs=(hbm,) * 5,
+        scratch_shapes=[V(out.shape, F32) for out in outs] + [S((2, 5))],
     )(*results)
     return attended, grad_in.T, grad_query, grad_key, grad_value
 

time: 180 us -> 120 us (0.67)
  Pallas kernels: 179 us -> 119 us
    pallas_call x1, Pallas kernels: 61.7 us -> 2.4 us  [local(): pl.pallas_call(hand_over, out_shape=outs, in_specs=[hbm] * 5, out_specs=(...]
where the time goes in v2:
time: 120 us
  Pallas kernels  119 us (99%)
    pallas_call x1, Pallas kernels, local(): pl.pallas_call(kernel, out_shape=outs, in_specs=[hbm] * 5 + [vmem] * 4, o...  117 us
    pallas_call x1, Pallas kernels, local(): pl.pallas_call(hand_over, out_shape=outs, in_specs=[hbm] * 5, out_specs=(...  2.4 us

profile of v2, /device:TPU:0, one launch (start us, length us, event | category | flops | bytes accessed | tf_op | source)
XLA Modules:
  0.0 120.1 jit_solution(904530914832993990)
XLA Ops:
  0.6 116.9 %shard_map.128 = (f32[256,512]{1,0:T(8,128)}, f32[480,256]{1,0:T(8,128)}, f32[240,512]{1,0:T(8,128)}, f32[240,256]{1,0:T(8,128)}, f32[240,256]{1,0:T(8,128)}) custom-call(f32[256,3840]{1,0:T(8,128)} %hid_h.1, f32[3840,512]{1,0:T(8,128)} %wq_h.1, f32[3840,256]{1,0:T(8,128)} %wk_h.1, f32[3840,256]{1,0:T(8,128)} %wv_h.1, f32[256,512]{1,0:T(8,128)} %grad_h.1, ...), custom_call_target="tpu_custom_call" | custom-call | flops 24000000000 | bytes 40000000 | tf_op jit(solution)/shard_map/pallas_call | solution.py:437
  117.5 2.4 %shard_map.129 = (f32[256,512]{1,0:T(8,128)}, f32[480,256]{1,0:T(8,128)}, f32[240,512]{1,0:T(8,128)}, f32[240,256]{1,0:T(8,128)}, f32[240,256]{1,0:T(8,128)}) custom-call(f32[256,512]{1,0:T(8,128)} %get-tuple-element.15.refs_0_, f32[480,256]{1,0:T(8,128)} %get-tuple-element.16.refs_1_, f32[240,512]{1,0:T(8,128)} %get-tuple-element.17.refs_2_, ...), custom_call_target="tpu_custom_call" | custom-call | tf_op jit(solution)/shard_map/pallas_call | solution.py:457

commit v3 on v2

--- a/solution.py
+++ b/solution.py
@@ -84,7 +84,7 @@
     hid_h, wq_h, wk_h, wv_h, grad_h, q_gain_r, k_gain_r, seg, freq_r,
     att_o, gin_o, gq_o, gk_o, gv_o,
     hid, wq, wk, wv, grad, raw, q2, kv, wt, dpt, dqt, contrib, rkv, prev, zr,
-    hz, ht_h, ht_l, dc, part, fwd, rpart, term, r1, r2, lsem, send_sems, recv_sems,
+    hz, ht_h, ht_l, dc, part, fwd, rpart, term, r1, r2, xfwd, lsem, osem, send_sems, recv_sems,
 ):
     s = lax.axis_index("seq")
     t = lax.axis_index("tensor")
@@ -112,19 +112,26 @@
     def first_col(zz):
         return ((15 * zz) // 2) * 128
 
+    pieces_of = {0: (pl.ds(0, 128), pl.ds(128, 128)), 1: (pl.ds(0, T),)}
     for kind in (0, 1):
-        links.add(("kv", 4, kind), kv.at[0, kind], kv.at[4, kind], at_z(1))
+        for i, rows in enumerate(pieces_of[kind]):
+            links.add(("kv", 4, kind, i), kv.at[0, kind, rows], kv.at[4, kind, rows], at_z(1))
+            for d in (1, 2, 3):
+                src = kv.at[4 * ((y + d) // 4), kind, rows]
+                links.add(("kv", d, kind, i), src, kv.at[d, kind, rows], at_y(d))
         links.add(("prev", kind), prev.at[kind], zr.at[kind], at_z(-1))
         for d in (1, 2, 3):
-            links.add(("kv", d, kind), kv.at[4 * ((y + d) // 4), kind], kv.at[d, kind], at_y(d))
             links.add(("back", d, kind), contrib.at[d, kind], rkv.at[d - 1, kind], at_y(-d))
     for d in (1, 2, 3):
         cols = pl.ds(pl.multiple_of(first_col(lax.rem(z + d, 4)), 128), 1024)
         links.add(("hid", d), hid.at[half, cols], hz.at[d - 1, half], at_z(d))
         links.add(("hid_mate", d), hz.at[d - 1, half], hz.at[d - 1, half], mate)
-        links.add(("x", d), term.at[0, d], r2.at[d - 1], at_x(d))
     for k in range(4):
         links.add(("core", k), term.at[1, k], r1.at[k], mate)
+    for i, d in enumerate((1, 3)):
+        rows = pl.ds(240 * i, 240)
+        links.add(("x_fwd", d), term.at[0, 2, rows], xfwd.at[i], at_x(d))
+        links.add(("x", d), term.at[0, d], r2.at[i], at_x(d))
     spans = {"q": pl.ds(0, 2 * H), "k": pl.ds(2 * H, H), "v": pl.ds(3 * H, H)}
     for g, cols in spans.items():
         links.add(("dc", g, 1), dc.at[0, :, cols], dc.at[1, :, cols], at_z(1))
@@ -137,6 +144,13 @@
         links.add(("sum", g, 1), part.at[1, g], rpart.at[0, g], at_y(1))
         links.add(("sum", g, 3), part.at[3, g], rpart.at[1, g], at_y(-1))
 
+    writes = []
+
+    def write(i, src, dst):
+        copy = pltpu.make_async_copy(src, dst, osem.at[i])
+        copy.start()
+        writes.append(copy)
+
     def columns(i):
         return pl.ds(pl.multiple_of(i * CH, CH), CH)
 
@@ -173,18 +187,26 @@
         return lax.fori_loop(0, NCH, step, jnp.zeros((T, H), F32))
 
     def send_own(kind):
-        links.start("kv", 4, kind)
+        for i in range(len(pieces_of[kind])):
+            links.start("kv", 4, kind, i)
         for d in (1, 2, 3):
             @pl.when(y + d < 4)
             def _():
-                links.start("kv", d, kind)
+                for i in range(len(pieces_of[kind])):
+                    links.start("kv", d, kind, i)
 
     def send_prev(kind):
-        links.arrived("kv", 4, kind)
-        for d in (1, 2, 3):
-            @pl.when(y + d >= 4)
-            def _():
-                links.start("kv", d, kind)
+        for i in range(len(pieces_of[kind])):
+            links.arrived("kv", 4, kind, i)
+            for d in (1, 2, 3):
+                @pl.when(y + d >= 4)
+                def _():
+                    links.start("kv", d, kind, i)
+
+    def have(d, kind):
+        if d in (1, 2, 3):
+            for i in range(len(pieces_of[kind])):
+                links.arrived("kv", d, kind, i)
 
     key_raw = project(1, wk, 0, True, True)
     raw[2] = key_raw
@@ -223,7 +245,7 @@
     seg_q = segments(s)
     seg_q = jnp.concatenate([seg_q, seg_q], axis=1)
 
-    def forward(d, total, delta):
+    def weigh(d):
         seg_k = jnp.broadcast_to(segments(lax.rem(s - d + 16, 16)), (T, T)).T
         seg_k = jnp.concatenate([seg_k, seg_k], axis=1)
         dist = 256 * d + col - row
@@ -231,20 +253,20 @@
         scores = product(split(kv[d, 0]), q_pair(), NT)
         weights = jnp.where(allowed, jnp.exp(scores), 0.0)
         wt[d] = weights
+        return jnp.sum(weights, axis=0, keepdims=True)
+
+    def weigh_values(d):
         d_shares = product(split(kv[d, 1]), g_pair(), NT)
         dpt[d] = d_shares
-        total = total + jnp.sum(weights, axis=0, keepdims=True)
-        delta = delta + jnp.sum(weights * d_shares, axis=0, keepdims=True)
-        return total, delta
+        return jnp.sum(wt[d] * d_shares, axis=0, keepdims=True)
 
     total = delta = jnp.zeros((1, 2 * T), F32)
-    for d in (0, 4, 1, 3, 2):
-        if d in (1, 2, 3):
-            links.arrived("kv", d, 0)
-            links.arrived("kv", d, 1)
-        total, delta = forward(d, total, delta)
+    for d in (0, 4):
+        total = total + weigh(d)
+    for d in (1, 3, 2):
+        have(d, 0)
+        total = total + weigh(d)
     inverse = 1.0 / total
-    delta = delta * inverse
 
     def back_values(d):
         shares = wt[d] * inverse
@@ -262,11 +284,14 @@
     for d in (2, 1, 3):
         back_values(d)
         links.start("back", d, 1)
-    for d in (2, 1, 3):
-        back_keys(d, d == 2)
     for d in (4, 0):
         back_values(d)
-        back_keys(d, False)
+        delta = delta + weigh_values(d)
+    for d in (1, 3, 2):
+        have(d, 1)
+        delta = delta + weigh_values(d)
+    for d in (2, 1, 3, 4, 0):
+        back_keys(d, d == 2)
     d_q = dqt[...].T * (H ** -0.5)
     for h in (0, 1):
         dc[0, :, h * H : (h + 1) * H] = norm_back(raw[h], q_gain, unrotate(d_q[h * T : (h + 1) * T], cos, sin))
@@ -290,9 +315,9 @@
     for d in range(5):
         more = product(split(kv[d, 1]), split(wt[d]), TN)
         out_t = more if out_t is None else out_t + more
-    attended = out_t.T
-    att_o[:, :H] = attended[:T]
-    att_o[:, H:] = attended[T:]
+    q2[...] = out_t.T
+    for h in (0, 1):
+        write(h, q2.at[h * T : (h + 1) * T], att_o.at[:, h * H : (h + 1) * H])
 
     for d in (1, 2, 3):
         links.arrived("hid", d)
@@ -313,6 +338,22 @@
     for d in (1, 2, 3):
         links.arrived("hid_mate", d)
         transpose_into(d, lambda lanes: hz[d - 1, :, pl.ds(lanes, 256)])
+
+    weights = [(wq, 0), (wq, H), (wk, 0), (wv, 0)]
+
+    def input_part(k, core, grads):
+        rows = pl.ds(pl.multiple_of((2 * lax.rem(x + k, 4) + core) * 480, 32), 480)
+        acc = None
+        for g, grad_g in grads.items():
+            w, first = weights[g]
+            one = product(split(w[rows, first : first + H]), grad_g, NT)
+            acc = one if acc is None else acc + one
+        return acc
+
+    q_own = {g: split(dc[0, :, g * H : (g + 1) * H]) for g in (0, 1)}
+    for k in range(4):
+        term[0, k] = input_part(k, c, q_own)
+        term[1, k] = input_part(k, 1 - c, q_own)
 
     def collect(kind):
         mine, before = contrib[0, kind], contrib[4, kind]
@@ -353,7 +394,9 @@
     def summed(g):
         links.arrived("sum", g, 1)
         links.arrived("sum", g, 3)
-        return part[0, g] + (rpart[0, g] + rpart[1, g])
+        part[0, g] = part[0, g] + (rpart[0, g] + rpart[1, g])
+        dst = (gq_o.at[:, :H], gq_o.at[:, H:], gk_o, gv_o)[g]
+        write(2 + g, part.at[0, g], dst)
 
     gathered("q")
     partial(0)
@@ -362,53 +405,58 @@
     links.arrived("prev", 1)
     dc[0, :, 3 * H : 4 * H] = contrib[0, 1] + zr[1]
     spread("v")
-    pass_on(0)
-    pass_on(1)
     links.arrived("prev", 0)
     d_key = unrotate(contrib[0, 0] + zr[0], cos, sin)
     dc[0, :, 2 * H : 3 * H] = norm_back(raw[2], k_gain, d_key)
     spread("k")
-
-    d_own = [split(dc[0, :, g * H : (g + 1) * H]) for g in range(4)]
-    weights = [(wq, 0), (wq, H), (wk, 0), (wv, 0)]
-
-    def input_term(tt):
-        rows = pl.ds(pl.multiple_of(tt * 480, 32), 480)
-        acc = None
-        for g in range(4):
-            w, first = weights[g]
-            one = product(split(w[rows, first : first + H]), d_own[g], NT)
-            acc = one if acc is None else acc + one
-        return acc
-
-    for k in (1, 2, 3, 0):
-        term[1, k] = input_term(2 * lax.rem(x + k, 4) + 1 - c)
+    pass_on(0)
+    pass_on(1)
+
+    kv_own = {g: split(dc[0, :, g * H : (g + 1) * H]) for g in (2, 3)}
+
+    def other(k):
+        term[1, k] = term[1, k] + input_part(k, 1 - c, kv_own)
         links.start("core", k)
-    spread_on("v")
-    for k in (1, 2, 3, 0):
-        mine = input_term(2 * lax.rem(x + k, 4) + c)
+
+    def both(k):
+        mine = term[0, k] + input_part(k, c, kv_own)
         links.arrived("core", k)
         term[0, k] = mine + r1[k]
-        if k:
-            links.start("x", k)
-    spread_on("k")
+
+    other(2)
+    other(1)
+    both(2)
+    for d in (1, 3):
+        links.start("x_fwd", d)
+    spread_on("v")
+    other(3)
+    other(0)
+    for k in (1, 3, 0):
+        both(k)
 
     gathered("v")
     partial(3)
+    spread_on("k")
+    for i, d in enumerate((1, 3)):
+        links.arrived("x_fwd", d)
+        rows = pl.ds(240 * i, 240)
+        term[0, d, rows] = term[0, d, rows] + xfwd[i]
+        links.start("x", d)
     gathered("k")
     partial(2)
     pass_on(3)
     pass_on(2)
 
-    gq_o[:, :H] = summed(0)
-    gq_o[:, H:] = summed(1)
-    total_in = term[0, 0]
-    for k in (1, 2, 3):
-        links.arrived("x", k)
-        total_in = total_in + r2[k - 1]
-    gin_o[...] = total_in
-    gv_o[...] = summed(3)
-    gk_o[...] = summed(2)
+    summed(0)
+    summed(1)
+    links.arrived("x", 1)
+    links.arrived("x", 3)
+    term[0, 0] = term[0, 0] + (r2[0] + r2[1])
+    write(6, term.at[0, 0], gin_o)
+    summed(3)
+    summed(2)
+    for copy in writes:
+        copy.wait()
     links.finish()
 
 
@@ -438,15 +486,15 @@
         kernel,
         out_shape=outs,
         in_specs=[hbm] * 5 + [vmem] * 4,
-        out_specs=(vmem,) * 5,
+        out_specs=(hbm,) * 5,
         scratch_shapes=[
             V((T, D), F32), V((D, 512), F32), V((D, 256), F32), V((D, 256), F32), V((T, 512), F32),
             V((3, T, H), F32), V((2 * T, H), F32), V((5, 2, T, H), F32), V((5, T, 2 * T), F32), V((5, T, 2 * T), F32),
             V((H, 2 * T), F32), V((5, 2, T, H), F32), V((3, 2, T, H), F32), V((2, T, H), F32), V((2, T, H), F32),
             V((3, T, 1024), F32), V((1024, 1024), BF16), V((1024, 1024), BF16), V((4, T, 1024), F32),
             V((4, 4, 240, H), F32), V((2, 4, 120, H), F32), V((2, 4, 240, H), F32),
-            V((2, 4, 480, T), F32), V((4, 480, T), F32), V((3, 480, T), F32),
-            S((5, NCH)), S((COPIES,)), S((COPIES,)),
+            V((2, 4, 480, T), F32), V((4, 480, T), F32), V((2, 480, T), F32), V((2, 240, T), F32),
+            S((5, NCH)), S((7,)), S((COPIES,)), S((COPIES,)),
         ],
         compiler_params=pltpu.CompilerParams(collective_id=0, has_side_effects=True, vmem_limit_bytes=63 << 20),
         cost_estimate=pl.CostEstimate(flops=24_000_000_000, bytes_accessed=40_000_000, transcendentals=700_000),

time: 120 us -> 126 us (1.050); the launches traced: 120 us -> 124 us
  Pallas kernels: 119 us -> 123 us
    pallas_call x1, Pallas kernels: 117 us -> 121 us  [local(): pl.pallas_call(kernel, out_shape=outs, in_specs=[hbm] * 5 + [vmem] * 4, o...]
where the time goes in v3:
time: 126 us; the launch traced here: 124 us
  Pallas kernels  123 us (98%)
    pallas_call x1, Pallas kernels, local(): pl.pallas_call(kernel, out_shape=outs, in_specs=[hbm] * 5 + [vmem] * 4, o...  121 us

profile of v3, /device:TPU:0, one launch (start us, length us, event | category | flops | bytes accessed | tf_op | source)
XLA Modules:
  0.0 124.1 jit_solution(3849061730473672407)
XLA Ops:
  0.6 120.9 %shard_map.128 = (f32[256,512]{1,0:T(8,128)}, f32[480,256]{1,0:T(8,128)}, f32[240,512]{1,0:T(8,128)}, f32[240,256]{1,0:T(8,128)}, f32[240,256]{1,0:T(8,128)}) custom-call(f32[256,3840]{1,0:T(8,128)} %hid_h.1, f32[3840,512]{1,0:T(8,128)} %wq_h.1, f32[3840,256]{1,0:T(8,128)} %wk_h.1, f32[3840,256]{1,0:T(8,128)} %wv_h.1, f32[256,512]{1,0:T(8,128)} %grad_h.1, ...), custom_call_target="tpu_custom_call" | custom-call | flops 24000000000 | bytes 40000000 | tf_op jit(solution)/shard_map/pallas_call | solution.py:485
  121.6 2.4 %shard_map.129 = (f32[256,512]{1,0:T(8,128)}, f32[480,256]{1,0:T(8,128)}, f32[240,512]{1,0:T(8,128)}, f32[240,256]{1,0:T(8,128)}, f32[240,256]{1,0:T(8,128)}) custom-call(f32[256,512]{1,0:T(8,128)} %get-tuple-element.15.refs_0_, f32[480,256]{1,0:T(8,128)} %get-tuple-element.16.refs_1_, f32[240,512]{1,0:T(8,128)} %get-tuple-element.17.refs_2_, ...), custom_call_target="tpu_custom_call" | custom-call | tf_op jit(solution)/shard_map/pallas_call | solution.py:505

commit v4 on v3

--- a/solution.py
+++ b/solution.py
@@ -77,7 +77,7 @@
             copy.wait_send()
 
 
-COPIES = 64
+COPIES = 72
 
 
 def kernel(
@@ -132,7 +132,7 @@
         rows = pl.ds(240 * i, 240)
         links.add(("x_fwd", d), term.at[0, 2, rows], xfwd.at[i], at_x(d))
         links.add(("x", d), term.at[0, d], r2.at[i], at_x(d))
-    spans = {"q": pl.ds(0, 2 * H), "k": pl.ds(2 * H, H), "v": pl.ds(3 * H, H)}
+    spans = {"q0": pl.ds(0, H), "q1": pl.ds(H, H), "k": pl.ds(2 * H, H), "v": pl.ds(3 * H, H)}
     for g, cols in spans.items():
         links.add(("dc", g, 1), dc.at[0, :, cols], dc.at[1, :, cols], at_z(1))
         links.add(("dc", g, 3), dc.at[0, :, cols], dc.at[3, :, cols], at_z(-1))
@@ -263,10 +263,15 @@
     total = delta = jnp.zeros((1, 2 * T), F32)
     for d in (0, 4):
         total = total + weigh(d)
+    for d in (0, 4):
+        delta = delta + weigh_values(d)
     for d in (1, 3, 2):
         have(d, 0)
         total = total + weigh(d)
+        have(d, 1)
+        delta = delta + weigh_values(d)
     inverse = 1.0 / total
+    delta = delta * inverse
 
     def back_values(d):
         shares = wt[d] * inverse
@@ -284,18 +289,12 @@
     for d in (2, 1, 3):
         back_values(d)
         links.start("back", d, 1)
+    for d in (2, 1, 3):
+        back_keys(d, d == 2)
     for d in (4, 0):
         back_values(d)
-        delta = delta + weigh_values(d)
-    for d in (1, 3, 2):
-        have(d, 1)
-        delta = delta + weigh_values(d)
-    for d in (2, 1, 3, 4, 0):
-        back_keys(d, d == 2)
+        back_keys(d, False)
     d_q = dqt[...].T * (H ** -0.5)
-    for h in (0, 1):
-        dc[0, :, h * H : (h + 1) * H] = norm_back(raw[h], q_gain, unrotate(d_q[h * T : (h + 1) * T], cos, sin))
-
     def spread(g):
         links.start("dc", g, 1)
         links.start("dc", g, 3)
@@ -309,7 +308,9 @@
         for d in (1, 3):
             links.arrived("dc2", g, d)
 
-    spread("q")
+    for h, g in ((0, "q0"), (1, "q1")):
+        dc[0, :, h * H : (h + 1) * H] = norm_back(raw[h], q_gain, unrotate(d_q[h * T : (h + 1) * T], cos, sin))
+        spread(g)
 
     out_t = None
     for d in range(5):
@@ -351,8 +352,11 @@
         return acc
 
     q_own = {g: split(dc[0, :, g * H : (g + 1) * H]) for g in (0, 1)}
+    spread_on("q0")
     for k in range(4):
         term[0, k] = input_part(k, c, q_own)
+        if k == 1:
+            spread_on("q1")
         term[1, k] = input_part(k, 1 - c, q_own)
 
     def collect(kind):
@@ -368,10 +372,12 @@
         links.start("prev", kind)
 
     collect(1)
-    spread_on("q")
-    collect(0)
 
     off = lax.rem(z, 2) * 64
+
+    def send_far(g):
+        links.start("fwd", g, 1)
+        links.start("fwd", g, 3)
 
     def partial(g):
         pieces = [split(dc[k, :, g * H : (g + 1) * H]) for k in range(4)]
@@ -379,9 +385,8 @@
         for d in (2, 1, 3, 0):
             rows = pl.ds(pl.multiple_of(off + 240 * lax.rem(y + d, 4), 16), 240)
             part[d, g] = product((ht_h[rows, :], ht_l[rows, :]), right, NN)
-            if d == 2:
-                links.start("fwd", g, 1)
-                links.start("fwd", g, 3)
+            if d == 2 and g > 1:
+                send_far(g)
 
     def pass_on(g):
         links.arrived("fwd", g, 1)
@@ -398,9 +403,13 @@
         dst = (gq_o.at[:, :H], gq_o.at[:, H:], gk_o, gv_o)[g]
         write(2 + g, part.at[0, g], dst)
 
-    gathered("q")
+    gathered("q0")
     partial(0)
+    gathered("q1")
     partial(1)
+    collect(0)
+    send_far(0)
+    send_far(1)
 
     links.arrived("prev", 1)
     dc[0, :, 3 * H : 4 * H] = contrib[0, 1] + zr[1]

time: 126 us -> 118 us (0.937)
  Pallas kernels: 123 us -> 115 us
    pallas_call x1, Pallas kernels: 121 us -> 113 us  [local(): pl.pallas_call(kernel, out_shape=outs, in_specs=[hbm] * 5 + [vmem] * 4, o...]
where the time goes in v4:
time: 118 us; the launch traced here: 116 us
  Pallas kernels  115 us (97%)
    pallas_call x1, Pallas kernels, local(): pl.pallas_call(kernel, out_shape=outs, in_specs=[hbm] * 5 + [vmem] * 4, o...  113 us
    pallas_call x1, Pallas kernels, local(): pl.pallas_call(hand_over, out_shape=outs, in_specs=[hbm] * 5, out_specs=(...  2.4 us

profile of v4, /device:TPU:0, one launch (start us, length us, event | category | flops | bytes accessed | tf_op | source)
XLA Modules:
  0.0 116.2 jit_solution(17809453385815008120)
XLA Ops:
  0.6 112.9 %shard_map.128 = (f32[256,512]{1,0:T(8,128)}, f32[480,256]{1,0:T(8,128)}, f32[240,512]{1,0:T(8,128)}, f32[240,256]{1,0:T(8,128)}, f32[240,256]{1,0:T(8,128)}) custom-call(f32[256,3840]{1,0:T(8,128)} %hid_h.1, f32[3840,512]{1,0:T(8,128)} %wq_h.1, f32[3840,256]{1,0:T(8,128)} %wk_h.1, f32[3840,256]{1,0:T(8,128)} %wv_h.1, f32[256,512]{1,0:T(8,128)} %grad_h.1, ...), custom_call_target="tpu_custom_call" | custom-call | flops 24000000000 | bytes 40000000 | tf_op jit(solution)/shard_map/pallas_call | solution.py:494
  113.6 2.4 %shard_map.129 = (f32[256,512]{1,0:T(8,128)}, f32[480,256]{1,0:T(8,128)}, f32[240,512]{1,0:T(8,128)}, f32[240,256]{1,0:T(8,128)}, f32[240,256]{1,0:T(8,128)}) custom-call(f32[256,512]{1,0:T(8,128)} %get-tuple-element.15.refs_0_, f32[480,256]{1,0:T(8,128)} %get-tuple-element.16.refs_1_, f32[240,512]{1,0:T(8,128)} %get-tuple-element.17.refs_2_, ...), custom_call_target="tpu_custom_call" | custom-call | tf_op jit(solution)/shard_map/pallas_call | solution.py:514

commit v5 on v4

--- a/solution.py
+++ b/solution.py
@@ -136,8 +136,9 @@
     for g, cols in spans.items():
         links.add(("dc", g, 1), dc.at[0, :, cols], dc.at[1, :, cols], at_z(1))
         links.add(("dc", g, 3), dc.at[0, :, cols], dc.at[3, :, cols], at_z(-1))
-        links.add(("dc2", g, 1), dc.at[1, :128, cols], dc.at[2, :128, cols], at_z(1))
-        links.add(("dc2", g, 3), dc.at[3, 128:, cols], dc.at[2, 128:, cols], at_z(-1))
+        cut = 128 if g in ("q0", "q1") else 192
+        links.add(("dc2", g, 1), dc.at[1, :cut, cols], dc.at[2, :cut, cols], at_z(1))
+        links.add(("dc2", g, 3), dc.at[3, cut:, cols], dc.at[2, cut:, cols], at_z(-1))
     for g in range(4):
         links.add(("fwd", g, 1), part.at[2, g, :120], fwd.at[0, g], at_y(1))
         links.add(("fwd", g, 3), part.at[2, g, 120:], fwd.at[1, g], at_y(-1))
@@ -278,23 +279,25 @@
         wt[d] = shares
         contrib[d, 1] = product(split(shares), g_pair(), NN)
 
-    def back_keys(d, first):
-        d_scores = split(wt[d] * (dpt[d] - delta))
-        contrib[d, 0] = product(d_scores, q_pair(), NN)
+    def back_scores(d):
+        d_scores = wt[d] * (dpt[d] - delta)
+        dpt[d] = d_scores
+        return product(split(kv[d, 0]), split(d_scores), TN)
+
+    def back_keys(d):
+        contrib[d, 0] = product(split(dpt[d]), q_pair(), NN)
         if d in (1, 2, 3):
             links.start("back", d, 0)
-        more = product(split(kv[d, 0]), d_scores, TN)
-        dqt[...] = more if first else dqt[...] + more
 
     for d in (2, 1, 3):
         back_values(d)
         links.start("back", d, 1)
-    for d in (2, 1, 3):
-        back_keys(d, d == 2)
     for d in (4, 0):
-        back_values(d)
-        back_keys(d, False)
-    d_q = dqt[...].T * (H ** -0.5)
+        wt[d] = wt[d] * inverse
+    dqt[...] = back_scores(0)
+    for d in (1, 2, 3, 4):
+        dqt[...] = dqt[...] + back_scores(d)
+
     def spread(g):
         links.start("dc", g, 1)
         links.start("dc", g, 3)
@@ -309,8 +312,14 @@
             links.arrived("dc2", g, d)
 
     for h, g in ((0, "q0"), (1, "q1")):
-        dc[0, :, h * H : (h + 1) * H] = norm_back(raw[h], q_gain, unrotate(d_q[h * T : (h + 1) * T], cos, sin))
+        d_q = dqt[:, h * T : (h + 1) * T].T * (H ** -0.5)
+        dc[0, :, h * H : (h + 1) * H] = norm_back(raw[h], q_gain, unrotate(d_q, cos, sin))
         spread(g)
+    for d in (2, 1, 3):
+        back_keys(d)
+    for d in (4, 0):
+        contrib[d, 1] = product(split(wt[d]), g_pair(), NN)
+        back_keys(d)
 
     out_t = None
     for d in range(5):

time: 118 us -> 116 us (0.983)
  Pallas kernels: 115 us -> 113 us
    pallas_call x1, Pallas kernels: 113 us -> 111 us  [local(): pl.pallas_call(kernel, out_shape=outs, in_specs=[hbm] * 5 + [vmem] * 4, o...]
where the time goes in v5:
time: 116 us; the launch traced here: 114 us
  Pallas kernels  113 us (97%)
    pallas_call x1, Pallas kernels, local(): pl.pallas_call(kernel, out_shape=outs, in_specs=[hbm] * 5 + [vmem] * 4, o...  111 us
    pallas_call x1, Pallas kernels, local(): pl.pallas_call(hand_over, out_shape=outs, in_specs=[hbm] * 5, out_specs=(...  2.4 us

profile of v5, /device:TPU:0, one launch (start us, length us, event | category | flops | bytes accessed | tf_op | source)
XLA Modules:
  0.0 114.0 jit_solution(11288430080533805582)
XLA Ops:
  0.6 110.8 %shard_map.128 = (f32[256,512]{1,0:T(8,128)}, f32[480,256]{1,0:T(8,128)}, f32[240,512]{1,0:T(8,128)}, f32[240,256]{1,0:T(8,128)}, f32[240,256]{1,0:T(8,128)}) custom-call(f32[256,3840]{1,0:T(8,128)} %hid_h.1, f32[3840,512]{1,0:T(8,128)} %wq_h.1, f32[3840,256]{1,0:T(8,128)} %wk_h.1, f32[3840,256]{1,0:T(8,128)} %wv_h.1, f32[256,512]{1,0:T(8,128)} %grad_h.1, ...), custom_call_target="tpu_custom_call" | custom-call | flops 24000000000 | bytes 40000000 | tf_op jit(solution)/shard_map/pallas_call | solution.py:503
  111.4 2.4 %shard_map.129 = (f32[256,512]{1,0:T(8,128)}, f32[480,256]{1,0:T(8,128)}, f32[240,512]{1,0:T(8,128)}, f32[240,256]{1,0:T(8,128)}, f32[240,256]{1,0:T(8,128)}) custom-call(f32[256,512]{1,0:T(8,128)} %get-tuple-element.15.refs_0_, f32[480,256]{1,0:T(8,128)} %get-tuple-element.16.refs_1_, f32[240,512]{1,0:T(8,128)} %get-tuple-element.17.refs_2_, ...), custom_call_target="tpu_custom_call" | custom-call | tf_op jit(solution)/shard_map/pallas_call | solution.py:523

commit v6 on v5

--- a/solution.py
+++ b/solution.py
@@ -231,6 +231,16 @@
     for d in (1, 2, 3):
         links.start("hid", d)
 
+    def transpose_into(d, read):
+        def step(i, carry):
+            lanes = pl.multiple_of(i * 256, 256)
+            high, low = split(read(lanes).T)
+            ht_h[pl.ds(lanes, 256), d * T : (d + 1) * T] = high
+            ht_l[pl.ds(lanes, 256), d * T : (d + 1) * T] = low
+            return carry
+
+        lax.fori_loop(0, 4, step, 0)
+
     def q_pair():
         return split(q2[...])
 
@@ -266,6 +276,8 @@
         total = total + weigh(d)
     for d in (0, 4):
         delta = delta + weigh_values(d)
+    base = first_col(z)
+    transpose_into(0, lambda lanes: hid[:, pl.ds(pl.multiple_of(base + lanes, 128), 256)])
     for d in (1, 3, 2):
         have(d, 0)
         total = total + weigh(d)
@@ -333,19 +345,9 @@
         links.arrived("hid", d)
         links.start("hid_mate", d)
 
-    def transpose_into(d, read):
-        def step(i, carry):
-            lanes = pl.multiple_of(i * 256, 256)
-            high, low = split(read(lanes).T)
-            ht_h[pl.ds(lanes, 256), d * T : (d + 1) * T] = high
-            ht_l[pl.ds(lanes, 256), d * T : (d + 1) * T] = low
-            return carry
-
-        lax.fori_loop(0, 4, step, 0)
-
-    base = first_col(z)
-    transpose_into(0, lambda lanes: hid[:, pl.ds(pl.multiple_of(base + lanes, 128), 256)])
     for d in (1, 2, 3):
+        if d == 3:
+            spread_on("q0")
         links.arrived("hid_mate", d)
         transpose_into(d, lambda lanes: hz[d - 1, :, pl.ds(lanes, 256)])
 
@@ -361,7 +363,6 @@
         return acc
 
     q_own = {g: split(dc[0, :, g * H : (g + 1) * H]) for g in (0, 1)}
-    spread_on("q0")
     for k in range(4):
         term[0, k] = input_part(k, c, q_own)
         if k == 1:

time: 116 us -> 116 us (level)
  no operation moved by 1% of the time
where the time goes in v6:
time: 116 us; the launch traced here: 114 us
  Pallas kernels  113 us (97%)
    pallas_call x1, Pallas kernels, local(): pl.pallas_call(kernel, out_shape=outs, in_specs=[hbm] * 5 + [vmem] * 4, o...  111 us
    pallas_call x1, Pallas kernels, local(): pl.pallas_call(hand_over, out_shape=outs, in_specs=[hbm] * 5, out_specs=(...  2.4 us

profile of v6, /device:TPU:0, one launch (start us, length us, event | category | flops | bytes accessed | tf_op | source)
XLA Modules:
  0.0 114.0 jit_solution(18198438922688820439)
XLA Ops:
  0.6 110.8 %shard_map.128 = (f32[256,512]{1,0:T(8,128)}, f32[480,256]{1,0:T(8,128)}, f32[240,512]{1,0:T(8,128)}, f32[240,256]{1,0:T(8,128)}, f32[240,256]{1,0:T(8,128)}) custom-call(f32[256,3840]{1,0:T(8,128)} %hid_h.1, f32[3840,512]{1,0:T(8,128)} %wq_h.1, f32[3840,256]{1,0:T(8,128)} %wk_h.1, f32[3840,256]{1,0:T(8,128)} %wv_h.1, f32[256,512]{1,0:T(8,128)} %grad_h.1, ...), custom_call_target="tpu_custom_call" | custom-call | flops 24000000000 | bytes 40000000 | tf_op jit(solution)/shard_map/pallas_call | solution.py:504
  111.4 2.4 %shard_map.129 = (f32[256,512]{1,0:T(8,128)}, f32[480,256]{1,0:T(8,128)}, f32[240,512]{1,0:T(8,128)}, f32[240,256]{1,0:T(8,128)}, f32[240,256]{1,0:T(8,128)}) custom-call(f32[256,512]{1,0:T(8,128)} %get-tuple-element.15.refs_0_, f32[480,256]{1,0:T(8,128)} %get-tuple-element.16.refs_1_, f32[240,512]{1,0:T(8,128)} %get-tuple-element.17.refs_2_, ...), custom_call_target="tpu_custom_call" | custom-call | tf_op jit(solution)/shard_map/pallas_call | solution.py:524

commit v7 on v6

--- a/solution.py
+++ b/solution.py
@@ -333,14 +333,6 @@
         contrib[d, 1] = product(split(wt[d]), g_pair(), NN)
         back_keys(d)
 
-    out_t = None
-    for d in range(5):
-        more = product(split(kv[d, 1]), split(wt[d]), TN)
-        out_t = more if out_t is None else out_t + more
-    q2[...] = out_t.T
-    for h in (0, 1):
-        write(h, q2.at[h * T : (h + 1) * T], att_o.at[:, h * H : (h + 1) * H])
-
     for d in (1, 2, 3):
         links.arrived("hid", d)
         links.start("hid_mate", d)
@@ -417,6 +409,14 @@
     partial(0)
     gathered("q1")
     partial(1)
+    out_t = None
+    for d in range(5):
+        more = product(split(kv[d, 1]), split(wt[d]), TN)
+        out_t = more if out_t is None else out_t + more
+    q2[...] = out_t.T
+    for h in (0, 1):
+        write(h, q2.at[h * T : (h + 1) * T], att_o.at[:, h * H : (h + 1) * H])
+
     collect(0)
     send_far(0)
     send_far(1)

time: 116 us -> 118 us (1.017)
  Pallas kernels: 113 us -> 116 us
    pallas_call x1, Pallas kernels: 111 us -> 114 us  [local(): pl.pallas_call(kernel, out_shape=outs, in_specs=[hbm] * 5 + [vmem] * 4, o...]
where the time goes in v7:
time: 118 us; the launch traced here: 117 us
  Pallas kernels  116 us (98%)
    pallas_call x1, Pallas kernels, local(): pl.pallas_call(kernel, out_shape=outs, in_specs=[hbm] * 5 + [vmem] * 4, o...  114 us
    pallas_call x1, Pallas kernels, local(): pl.pallas_call(hand_over, out_shape=outs, in_specs=[hbm] * 5, out_specs=(...  2.4 us

profile of v7, /device:TPU:0, one launch (start us, length us, event | category | flops | bytes accessed | tf_op | source)
XLA Modules:
  0.0 116.8 jit_solution(16419666445377569122)
XLA Ops:
  0.6 113.6 %shard_map.128 = (f32[256,512]{1,0:T(8,128)}, f32[480,256]{1,0:T(8,128)}, f32[240,512]{1,0:T(8,128)}, f32[240,256]{1,0:T(8,128)}, f32[240,256]{1,0:T(8,128)}) custom-call(f32[256,3840]{1,0:T(8,128)} %hid_h.1, f32[3840,512]{1,0:T(8,128)} %wq_h.1, f32[3840,256]{1,0:T(8,128)} %wk_h.1, f32[3840,256]{1,0:T(8,128)} %wv_h.1, f32[256,512]{1,0:T(8,128)} %grad_h.1, ...), custom_call_target="tpu_custom_call" | custom-call | flops 24000000000 | bytes 40000000 | tf_op jit(solution)/shard_map/pallas_call | solution.py:504
  114.2 2.4 %shard_map.129 = (f32[256,512]{1,0:T(8,128)}, f32[480,256]{1,0:T(8,128)}, f32[240,512]{1,0:T(8,128)}, f32[240,256]{1,0:T(8,128)}, f32[240,256]{1,0:T(8,128)}) custom-call(f32[256,512]{1,0:T(8,128)} %get-tuple-element.15.refs_0_, f32[480,256]{1,0:T(8,128)} %get-tuple-element.16.refs_1_, f32[240,512]{1,0:T(8,128)} %get-tuple-element.17.refs_2_, ...), custom_call_target="tpu_custom_call" | custom-call | tf_op jit(solution)/shard_map/pallas_call | solution.py:524
